TPU v7x, 32 devices: a whole 2x2x4 slice. The times are simulated.
32 devices in a mesh: section: 2 (over x), seq: 16 (over z, y, core).
Axes of the slice: x: 2, y: 2, z: 4, core: 2. Of those that a mesh axis runs over, the one named last changes fastest.
Arguments:
- prev_out: bfloat16 [2, 2048, 1792], P('section', 'seq'), may hold values from -6 to 6
- prev_grad: bfloat16 [2, 2048, 1792], P('section', 'seq'), may hold values from -6 to 6
- saved_in: bfloat16 [2, 2048, 1792], P('section', 'seq'), may hold values from -6 to 6
- seq_mix: bfloat16 [2, 128, 128], P('section'), may hold values from -0.5 to 0.5
- coeffs: float32 [2, 4, 4, 1792], P('section'), may hold values from -1 to 1
- mixer: bfloat16 [2, 1792, 448], P('section'), may hold values from -0.25 to 0.25
Outputs:
- out_fwd: bfloat16 [2, 2048, 1792], P('section', 'seq')
- out_dh: bfloat16 [2, 2048, 1792], P('section', 'seq')
- grad_w: float32 [2, 1792, 448], P('section', 'seq')
- grad_b: float32 [2, 128, 128], P('section')
All inputs are finite; a program needn't handle non-finite values.
Results may differ from a plain program's by a relative error of at most 0.01.
Values may be sent and summed in bfloat16 or wider, within the bound.
No kernel may reach another device: no remote copies, remote signals or barrier semaphores. Data moves between devices by JAX's collectives and lax.ppermute only.
A program may use at most 64 MiB of HBM per device.

v0:
```python
import jax
import jax.numpy as jnp
from jax import lax
from jax.sharding import PartitionSpec as P


def swapped(block, axis, stride):
    count = lax.axis_size(axis)
    route = []
    for low in range(count):
        high = low | 1 << stride
        if high != low and high < count:
            route += [(low, high), (high, low)]
    return lax.ppermute(block, axis, route)


def from_behind(block, axis, distance):
    devices = range(lax.axis_size(axis))
    route = [((i - distance) % len(devices), i) for i in devices]
    return lax.ppermute(block, axis, route)


def mix_forward(state, factors):
    position = lax.axis_index("seq")
    number = lax.axis_size("seq").bit_length() - 1
    for bit_level in range(number):
        partner = swapped(state, "seq", bit_level)
        upper_side = jnp.bitwise_and(jnp.right_shift(position, bit_level), 1) == 1
        own_vals = state.astype(jnp.float32)
        partner_vals = partner.astype(jnp.float32)
        as_lower = factors[bit_level, 0] * own_vals + factors[bit_level, 1] * partner_vals
        as_upper = factors[bit_level, 2] * partner_vals + factors[bit_level, 3] * own_vals
        state = jnp.where(upper_side, as_upper, as_lower).astype(jnp.bfloat16)
    return state


def mix_adjoint(state, factors):
    position = lax.axis_index("seq")
    number = lax.axis_size("seq").bit_length() - 1
    for bit_level in reversed(range(number)):
        partner = swapped(state, "seq", bit_level)
        upper_side = jnp.bitwise_and(jnp.right_shift(position, bit_level), 1) == 1
        own_vals = state.astype(jnp.float32)
        partner_vals = partner.astype(jnp.float32)
        as_lower = factors[bit_level, 0] * own_vals + factors[bit_level, 2] * partner_vals
        as_upper = factors[bit_level, 1] * partner_vals + factors[bit_level, 3] * own_vals
        state = jnp.where(upper_side, as_upper, as_lower).astype(jnp.bfloat16)
    return state


def block_apply(rows, blocks):
    block_len = blocks.shape[0]
    shaped = rows.reshape(-1, block_len, rows.shape[1])
    mixed = jnp.einsum("ij,bjd->bid", blocks, shaped, preferred_element_type=jnp.float32)
    return mixed.reshape(rows.shape).astype(jnp.bfloat16)


def layer_forward(rows, blocks, factors, weights):
    width = rows.shape[1]
    block_width = weights.shape[1]
    nblocks = width // block_width
    blocked = block_apply(rows, blocks)
    state = mix_forward(blocked, factors)
    act = (rows.astype(jnp.float32) + state.astype(jnp.float32)).astype(jnp.bfloat16)
    act3 = act.reshape(-1, nblocks, block_width)
    weight3 = weights.reshape(nblocks, block_width, block_width)
    pre = jnp.einsum("tbi,bio->tbo", act3, weight3, preferred_element_type=jnp.float32)
    return (act3, pre)


def on_device(prev_out, prev_grad, saved_in, seq_mix, coeffs, mixer):
    incoming = from_behind(prev_out, "section", 1)[0]
    upstream = from_behind(prev_grad, "section", -1)[0]
    blocks = seq_mix[0]
    factors = coeffs[0]
    weights = mixer[0]
    rows_dev, width = incoming.shape
    block_width = weights.shape[1]
    nblocks = width // block_width
    block_len = blocks.shape[0]
    act3, pre = layer_forward(incoming, blocks, factors, weights)
    result = (
        (act3.astype(jnp.float32) + jax.nn.silu(pre)).reshape(rows_dev, width).astype(jnp.bfloat16)
    )
    stored = saved_in[0]
    act_two, pre_two = layer_forward(stored, blocks, factors, weights)
    sigma = jax.nn.sigmoid(pre_two)
    gz = (
        upstream.astype(jnp.float32).reshape(-1, nblocks, block_width)
        * (sigma * (1.0 + pre_two * (1.0 - sigma)))
    ).astype(jnp.bfloat16)
    weight3 = weights.reshape(nblocks, block_width, block_width)
    back = jnp.einsum("tbo,bio->tbi", gz, weight3, preferred_element_type=jnp.float32)
    d_act = (upstream.astype(jnp.float32) + back.reshape(rows_dev, width)).astype(jnp.bfloat16)
    weight_term = jnp.einsum(
        "tbi,tbo->bio", act_two, gz, preferred_element_type=jnp.float32
    ).reshape(width, block_width)
    grad_weight = lax.psum_scatter(weight_term, "seq", scatter_dimension=0, tiled=True)
    dblocked = mix_adjoint(d_act, factors)
    dblk = dblocked.reshape(-1, block_len, width)
    stored_blk = stored.reshape(-1, block_len, width)
    block_term = jnp.einsum("bid,bjd->ij", dblk, stored_blk, preferred_element_type=jnp.float32)
    grad_block = lax.psum(block_term, "seq")
    through = jnp.einsum("ij,bid->bjd", blocks, dblk, preferred_element_type=jnp.float32).reshape(
        rows_dev, width
    )
    in_grad = (d_act.astype(jnp.float32) + through).astype(jnp.bfloat16)
    return (result[None], in_grad[None], grad_weight[None], grad_block[None])


def solution(mesh):
    placed = (
        P("section", "seq", None),
        P("section", "seq", None),
        P("section", "seq", None),
        P("section", None, None),
        P("section", None, None, None),
        P("section", None, None),
    )
    return jax.shard_map(
        on_device,
        mesh=mesh,
        in_specs=placed,
        out_specs=(
            P("section", "seq", None),
            P("section", "seq", None),
            P("section", "seq", None),
            P("section", None, None),
        ),
        check_vma=False,
    )
```

profile of v0, /device:TPU:0, one launch (start us, length us, event | category | flops | bytes accessed | tf_op | source)
XLA Modules:
  0.0 301.7 jit_solution(15228928650524788524)
XLA Ops:
  7.2 0.7 copy-done
  7.9 1.3 fusion.1
  9.8 1.3 slice_reduce_fusion.15
  11.2 1.3 fusion.20
  12.6 3.0 collective-permute-start.7
  15.5 10.8 %collective-permute-done.7 = bf16[128,1792]{0,1:T(8,128)(2,1)S(1)} collective-permute-done((bf16[128,1792]{0,1:T(8,128)(2,1)S(1)}, bf16[128,1792]{0,1:T(8,128)(2,1)S(1)}, u32[]{:S(2)}, u32[]{:S(2)}) %collective-permute-start.7) | collective-permute-done | bytes 458784 | tf_op jit(solution)/shard_map/ppermute | solution.py:14
  26.4 1.3 fusion.24
  27.7 1.9 collective-permute-start.8
  29.6 10.3 %collective-permute-done.8 = bf16[128,1792]{0,1:T(8,128)(2,1)S(1)} collective-permute-done((bf16[128,1792]{0,1:T(8,128)(2,1)S(1)}, bf16[128,1792]{0,1:T(8,128)(2,1)S(1)}, u32[]{:S(2)}, u32[]{:S(2)}) %collective-permute-start.8) | collective-permute-done | bytes 458784 | tf_op jit(solution)/shard_map/ppermute | solution.py:14
  39.8 1.3 fusion.28
  41.2 2.6 collective-permute-start.9
  43.7 1.0 copy.12
  44.7 1.5 collective-permute-start.5
  46.2 1.0 copy.13
  47.2 2.8 copy.18
  50.0 13.3 %collective-permute-done.9 = bf16[128,1792]{0,1:T(8,128)(2,1)} collective-permute-done((bf16[128,1792]{0,1:T(8,128)(2,1)S(1)}, bf16[128,1792]{0,1:T(8,128)(2,1)}, u32[]{:S(2)}, u32[]{:S(2)}) %collective-permute-start.9) | collective-permute-done | bytes 458784 | tf_op jit(solution)/shard_map/ppermute | solution.py:14
  63.2 3.0 add_convert_fusion.1
  66.2 0.8 convolution_bitcast_fusion.1
  67.1 0.7 fusion.59
  68.0 0.9 copy-done.4
  69.1 22.5 %collective-permute-done.10 = bf16[128,1792]{0,1:T(8,128)(2,1)S(1)} collective-permute-done((bf16[128,1792]{0,1:T(8,128)(2,1)S(1)}, bf16[128,1792]{0,1:T(8,128)(2,1)S(1)}, u32[]{:S(2)}, u32[]{:S(2)}) %collective-permute-start.10) | collective-permute-done | bytes 458784 | tf_op jit(solution)/shard_map/ppermute | solution.py:14
  91.6 2.2 fusion.36
  93.8 2.0 copy.10
  95.8 0.6 collective-permute-start
  96.4 9.0 %collective-permute-done.11 = bf16[128,1792]{0,1:T(8,128)(2,1)} collective-permute-done((bf16[128,1792]{0,1:T(8,128)(2,1)}, bf16[128,1792]{0,1:T(8,128)(2,1)}, u32[]{:S(2)}, u32[]{:S(2)}) %collective-permute-start.11) | collective-permute-done | bytes 458784 | tf_op jit(solution)/shard_map/ppermute | solution.py:14
  105.5 2.9 fusion.40
  108.8 10.0 %collective-permute-done.12 = bf16[128,1792]{0,1:T(8,128)(2,1)S(1)} collective-permute-done((bf16[128,1792]{0,1:T(8,128)(2,1)S(1)}, bf16[128,1792]{0,1:T(8,128)(2,1)S(1)}, u32[]{:S(2)}, u32[]{:S(2)}) %collective-permute-start.12) | collective-permute-done | bytes 458784 | tf_op jit(solution)/shard_map/ppermute | solution.py:14
  118.8 1.3 fusion.44
  120.3 1.8 collective-permute-done.13
  122.0 2.2 fusion.48
  124.3 0.8 copy-done.2
  125.0 1.0 convolution_bitcast_fusion.3
  126.3 3.7 %fusion.58 = f32[4,448,448]{2,1,0:T(8,128)} fusion(bf16[128,4,448]{0,2,1:T(8,128)(2,1)S(1)} %bitcast.83, f32[128,4,448]{0,2,1:T(8,128)} %copy-done.6, bf16[128,4,448]{0,2,1:T(8,128)(2,1)S(1)} %bitcast.81), kind=kOutput, calls=%fused_computation.135 | convolution fusion | flops 207814656 | bytes 5046272 | tf_op jit(solution)/shard_map/tbi,tbo->bio/dot_general | solution.py:95
  130.0 1.0 copy-done.9
  131.3 12.5 %collective-permute-done.2 = bf16[128,1792]{0,1:T(8,128)(2,1)S(1)} collective-permute-done((bf16[128,1792]{0,1:T(8,128)(2,1)S(1)}, bf16[128,1792]{0,1:T(8,128)(2,1)S(1)}, u32[]{:S(2)}, u32[]{:S(2)}) %collective-permute-start.2) | collective-permute-done | bytes 458784 | tf_op jit(solution)/shard_map/ppermute | solution.py:14
  143.7 1.3 fusion.8
  145.1 0.6 collective-permute-start.3
  146.0 11.1 %collective-permute-done.3 = bf16[128,1792]{0,1:T(8,128)(2,1)S(1)} collective-permute-done((bf16[128,1792]{0,1:T(8,128)(2,1)S(1)}, bf16[128,1792]{0,1:T(8,128)(2,1)S(1)}, u32[]{:S(2)}, u32[]{:S(2)}) %collective-permute-start.3) | collective-permute-done | bytes 458784 | tf_op jit(solution)/shard_map/ppermute | solution.py:14
  157.1 2.2 fusion.12
  159.3 2.6 collective-permute-start.4
  162.1 1.0 copy.17
  163.1 18.6 %collective-permute-done.4 = bf16[128,1792]{0,1:T(8,128)(2,1)} collective-permute-done((bf16[128,1792]{0,1:T(8,128)(2,1)}, bf16[128,1792]{0,1:T(8,128)(2,1)}, u32[]{:S(2)}, u32[]{:S(2)}) %collective-permute-start.4) | collective-permute-done | bytes 458784 | tf_op jit(solution)/shard_map/ppermute | solution.py:14
  181.7 2.9 add_convert_fusion.3
  184.5 0.9 add_convert_fusion.2
  185.4 1.0 copy.16
  186.4 31.9 %all-reduce.2.cloned.1.call-done = f32[1,128,128]{2,1,0:T(8,128)} async-done(((f32[1,128,128]{2,1,0:T(8,128)}), f32[1,128,128]{2,1,0:T(8,128)}) %all-reduce.2.cloned.1.call-update) | async-done | bytes 65552 | tf_op jit(solution)/shard_map/psum | solution.py:103
  218.3 75.1 %reduce-scatter.2.cloned.1.call-done = f32[112,448]{1,0:T(8,128)} async-done(((f32[1792,448]{1,0:T(8,128)}), f32[112,448]{1,0:T(8,128)}) %reduce-scatter.2.cloned.1.call-update) | async-done | bytes 200720 | tf_op jit(solution)/shard_map/reduce_scatter | solution.py:98
  293.4 1.5 copy.20
  (39 shorter events, 2.5 us)
Async XLA Ops:
  7.2 0.8 copy-start
  7.2 211.1 %all-reduce.2.cloned.1.call-start = ((), (), s32[]{:S(2)}) async-start(), calls=%async_computation.2 | async-start | bytes 131072 | tf_op jit(solution)/shard_map/psum | solution.py:103
  9.3 2.0 collective-permute-start.6
  11.2 32.5 %copy-start.11 = (bf16[1,128,1792]{2,1,0:T(8,128)(2,1)S(1)}, bf16[1,128,1792]{2,1,0:T(8,128)(2,1)}, u32[]{:S(2)}) copy-start(bf16[1,128,1792]{2,1,0:T(8,128)(2,1)} %param.7) | copy-start | bytes 1376260
  12.6 13.8 %collective-permute-start.7 = (bf16[128,1792]{0,1:T(8,128)(2,1)S(1)}, bf16[128,1792]{0,1:T(8,128)(2,1)S(1)}, u32[]{:S(2)}, u32[]{:S(2)}) collective-permute-start(bf16[128,1792]{0,1:T(8,128)(2,1)S(1)} %fusion.20), channel_id=1, source_target_pairs={{0,2},{2,0},{1,3},{3,1},{4,6},{6,4},{5,7},{7,5},{8,10},{10,8},{9,1... | collective-permute-start | bytes 1376264 | tf_op jit(solution)/shard_map/ppermute | solution.py:14
  26.3 19.9 %copy-start.1 = (bf16[1,128,1792]{2,1,0:T(8,128)(2,1)S(1)}, bf16[1,128,1792]{2,1,0:T(8,128)(2,1)}, u32[]{:S(2)}) copy-start(bf16[1,128,1792]{2,1,0:T(8,128)(2,1)} %param.8) | copy-start | bytes 1376260
  27.7 12.1 %collective-permute-start.8 = (bf16[128,1792]{0,1:T(8,128)(2,1)S(1)}, bf16[128,1792]{0,1:T(8,128)(2,1)S(1)}, u32[]{:S(2)}, u32[]{:S(2)}) collective-permute-start(bf16[128,1792]{0,1:T(8,128)(2,1)S(1)} %fusion.24), channel_id=1, source_target_pairs={{0,4},{4,0},{1,5},{5,1},{2,6},{6,2},{3,7},{7,3},{8,12},{12,8},{9,1... | collective-permute-start | bytes 1376264 | tf_op jit(solution)/shard_map/ppermute | solution.py:14
  41.2 8.8 %copy-start.10 = (bf16[128,1792]{0,1:T(8,128)(2,1)}, bf16[128,1792]{0,1:T(8,128)(2,1)S(1)}, u32[]{:S(2)}) copy-start(bf16[128,1792]{0,1:T(8,128)(2,1)S(1)} %fusion.28) | copy-start | bytes 1376260
  41.2 22.1 %collective-permute-start.9 = (bf16[128,1792]{0,1:T(8,128)(2,1)S(1)}, bf16[128,1792]{0,1:T(8,128)(2,1)}, u32[]{:S(2)}, u32[]{:S(2)}) collective-permute-start(bf16[128,1792]{0,1:T(8,128)(2,1)S(1)} %fusion.28), channel_id=1, source_target_pairs={{0,8},{8,0},{1,9},{9,1},{2,10},{10,2},{3,11},{11,3},{4,12},{12,4},... | collective-permute-start | bytes 1376264 | tf_op jit(solution)/shard_map/ppermute | solution.py:14
  44.7 22.4 %collective-permute-start.5 = (bf16[1,128,1792]{1,2,0:T(8,128)(2,1)}, bf16[1,128,1792]{1,2,0:T(8,128)(2,1)S(1)}, u32[]{:S(2)}, u32[]{:S(2)}) collective-permute-start(bf16[1,128,1792]{1,2,0:T(8,128)(2,1)} %copy.12), channel_id=1, source_target_pairs={{16,0},{0,16},{17,1},{1,17},{18,2},{2,18},{19,3},{3,19},{20,4},{4,... | collective-permute-start | bytes 1376264 | tf_op jit(solution)/shard_map/ppermute | solution.py:20
  67.1 0.9 copy-start.6
  68.0 0.9 copy-start.4
  69.0 22.6 %collective-permute-start.10 = (bf16[128,1792]{0,1:T(8,128)(2,1)S(1)}, bf16[128,1792]{0,1:T(8,128)(2,1)S(1)}, u32[]{:S(2)}, u32[]{:S(2)}) collective-permute-start(bf16[128,1792]{0,1:T(8,128)(2,1)S(1)} %fusion.50), channel_id=1, source_target_pairs={{0,8},{8,0},{1,9},{9,1},{2,10},{10,2},{3,11},{11,3},{4,12},{12,4},... | collective-permute-start | bytes 1376264 | tf_op jit(solution)/shard_map/ppermute | solution.py:14
  93.8 11.6 %collective-permute-start.11 = (bf16[128,1792]{0,1:T(8,128)(2,1)}, bf16[128,1792]{0,1:T(8,128)(2,1)}, u32[]{:S(2)}, u32[]{:S(2)}) collective-permute-start(bf16[128,1792]{0,1:T(8,128)(2,1)} %fusion.36), channel_id=1, source_target_pairs={{0,4},{4,0},{1,5},{5,1},{2,6},{6,2},{3,7},{7,3},{8,12},{12,8},{9,1... | collective-permute-start | bytes 1376264 | tf_op jit(solution)/shard_map/ppermute | solution.py:14
  95.8 12.6 %collective-permute-start = (bf16[1,128,1792]{1,2,0:T(8,128)(2,1)}, bf16[1,128,1792]{1,2,0:T(8,128)(2,1)S(1)}, u32[]{:S(2)}, u32[]{:S(2)}) collective-permute-start(bf16[1,128,1792]{1,2,0:T(8,128)(2,1)} %copy.10), channel_id=1, source_target_pairs={{16,0},{0,16},{17,1},{1,17},{18,2},{2,18},{19,3},{3,19},{20,4},{4,... | collective-permute-start | bytes 1376264 | tf_op jit(solution)/shard_map/ppermute | solution.py:20
  108.3 10.5 %collective-permute-start.12 = (bf16[128,1792]{0,1:T(8,128)(2,1)S(1)}, bf16[128,1792]{0,1:T(8,128)(2,1)S(1)}, u32[]{:S(2)}, u32[]{:S(2)}) collective-permute-start(bf16[128,1792]{0,1:T(8,128)(2,1)S(1)} %fusion.40), channel_id=1, source_target_pairs={{0,2},{2,0},{1,3},{3,1},{4,6},{6,4},{5,7},{7,5},{8,10},{10,8},{9,1... | collective-permute-start | bytes 1376264 | tf_op jit(solution)/shard_map/ppermute | solution.py:14
  108.4 11.8 %copy-start.7 = (bf16[1,128,1792]{1,2,0:T(8,128)(2,1)}, bf16[1,128,1792]{1,2,0:T(8,128)(2,1)S(1)}, u32[]{:S(2)}) copy-start(bf16[1,128,1792]{1,2,0:T(8,128)(2,1)S(1)} %collective-permute-done) | copy-start | bytes 1376260
  108.7 11.5 %collective-permute-start.1 = (bf16[128,1792]{0,1:T(8,128)(2,1)S(1)}, bf16[128,1792]{0,1:T(8,128)(2,1)S(1)}, u32[]{:S(2)}, u32[]{:S(2)}) collective-permute-start(bf16[128,1792]{0,1:T(8,128)(2,1)S(1)} %fusion), channel_id=1, source_target_pairs={{0,1},{1,0},{2,3},{3,2},{4,5},{5,4},{6,7},{7,6},{8,9},{9,8},{10,11... | collective-permute-start | bytes 1376264 | tf_op jit(solution)/shard_map/ppermute | solution.py:14
  120.2 1.9 collective-permute-start.13
  124.3 0.8 copy-start.2
  126.0 167.3 %reduce-scatter.2.cloned.1.call-start = ((), (), s32[]{:S(2)}) async-start(), calls=%async_computation.1 | async-start | bytes 3899392 | tf_op jit(solution)/shard_map/reduce_scatter | solution.py:98
  129.9 1.0 copy-start.9
  129.9 15.8 %copy-start.3 = (bf16[128,1792]{0,1:T(8,128)(2,1)S(1)}, bf16[128,1792]{0,1:T(8,128)(2,1)}, u32[]{:S(2)}) copy-start(bf16[128,1792]{0,1:T(8,128)(2,1)} %copy-done.2) | copy-start | bytes 1376260
  131.0 31.0 %copy-start.5 = (f32[4,128,448]{1,2,0:T(8,128)S(1)}, f32[4,128,448]{1,2,0:T(8,128)}, u32[]{:S(2)}) copy-start(f32[4,128,448]{1,2,0:T(8,128)} %copy-done.4) | copy-start | bytes 2752516
  131.0 12.8 %collective-permute-start.2 = (bf16[128,1792]{0,1:T(8,128)(2,1)S(1)}, bf16[128,1792]{0,1:T(8,128)(2,1)S(1)}, u32[]{:S(2)}, u32[]{:S(2)}) collective-permute-start(bf16[128,1792]{0,1:T(8,128)(2,1)S(1)} %copy-done.9), channel_id=1, source_target_pairs={{0,2},{2,0},{1,3},{3,1},{4,6},{6,4},{5,7},{7,5},{8,10},{10,8},{9,1... | collective-permute-start | bytes 1376264 | tf_op jit(solution)/shard_map/ppermute | solution.py:14
  145.1 12.0 %collective-permute-start.3 = (bf16[128,1792]{0,1:T(8,128)(2,1)S(1)}, bf16[128,1792]{0,1:T(8,128)(2,1)S(1)}, u32[]{:S(2)}, u32[]{:S(2)}) collective-permute-start(bf16[128,1792]{0,1:T(8,128)(2,1)S(1)} %fusion.8), channel_id=1, source_target_pairs={{0,4},{4,0},{1,5},{5,1},{2,6},{6,2},{3,7},{7,3},{8,12},{12,8},{9,1... | collective-permute-start | bytes 1376264 | tf_op jit(solution)/shard_map/ppermute | solution.py:14
  159.3 22.3 %collective-permute-start.4 = (bf16[128,1792]{0,1:T(8,128)(2,1)}, bf16[128,1792]{0,1:T(8,128)(2,1)}, u32[]{:S(2)}, u32[]{:S(2)}) collective-permute-start(bf16[128,1792]{0,1:T(8,128)(2,1)} %fusion.12), channel_id=1, source_target_pairs={{0,8},{8,0},{1,9},{9,1},{2,10},{10,2},{3,11},{11,3},{4,12},{12,4},... | collective-permute-start | bytes 1376264 | tf_op jit(solution)/shard_map/ppermute | solution.py:14
  161.9 19.7 %copy-start.8 = (bf16[1,128,1792]{1,2,0:T(8,128)(2,1)S(1)}, bf16[1,128,1792]{1,2,0:T(8,128)(2,1)}, u32[]{:S(2)}) copy-start(bf16[1,128,1792]{1,2,0:T(8,128)(2,1)} %copy-done.7) | copy-start | bytes 1376260
Sparse Core Ops, SparseCore 0:
  126.2 92.0 all-reduce.1
  223.2 70.1 reduce-scatter.1
where the time goes:
time: 302 us
  waiting for transfers between devices  227 us (75%)
  other arithmetic  22.3 us (7%)
  local copies, waits for them, and re-layouts  15.1 us (5%)
  between operations  14.3 us (5%)
  starting transfers between devices  14.1 us (5%)
  matrix products  8.92 us (3%)
    ppermute x12, waiting for transfers between devices, swapped(): return lax.ppermute(block, axis, route)  120 us
    reduce_scatter x1, waiting for transfers between devices, on_device(): lax.psum_scatter(weight_term, 'seq', scatter_dimension=0, tiled=True)  75.1 us
    psum x1, waiting for transfers between devices, on_device(): grad_block = lax.psum(block_term, 'seq')  31.9 us
    ppermute x12, starting transfers between devices, swapped(): return lax.ppermute(block, axis, route)  11.7 us
    unnamed x30, local copies, waits for them, and re-layouts  11 us
    convert_element_type x4, other arithmetic, mix_adjoint(): state = jnp.where(upper_side, as_upper, as_lower).astype(jnp.bfloat16)  8.65 us
    convert_element_type x5, other arithmetic, mix_forward(): state = jnp.where(upper_side, as_upper, as_lower).astype(jnp.bfloat16)  7.57 us
  transfers between devices with their start and end apart: 16, of which 13 were waited for; matrix products, arithmetic and copies ran while one was open for 10% of the time, Pallas kernels for 0%

commit v1 on v0

--- a/solution.py
+++ b/solution.py
@@ -2,6 +2,11 @@
 import jax.numpy as jnp
 from jax import lax
 from jax.sharding import PartitionSpec as P
+
+
+def add_all(x, axis):
+    parts = lax.all_gather(x, axis)
+    return jnp.sum(parts, axis=0)
 
 
 def swapped(block, axis, stride):
@@ -100,7 +105,7 @@
     dblk = dblocked.reshape(-1, block_len, width)
     stored_blk = stored.reshape(-1, block_len, width)
     block_term = jnp.einsum("bid,bjd->ij", dblk, stored_blk, preferred_element_type=jnp.float32)
-    grad_block = lax.psum(block_term, "seq")
+    grad_block = add_all(block_term, "seq")
     through = jnp.einsum("ij,bid->bjd", blocks, dblk, preferred_element_type=jnp.float32).reshape(
         rows_dev, width
     )

time: 302 us -> 245 us (0.81)
  waiting for transfers between devices: 227 us -> 168 us
    psum x1 -> x0, waiting for transfers between devices: 31.9 us -> none  [on_device(): grad_block = lax.psum(block_term, 'seq')]
    reduce_scatter x1, waiting for transfers between devices: 75.1 us -> 46.1 us  [on_device(): lax.psum_scatter(weight_term, 'seq', scatter_dimension=0, tiled=True)]
    unnamed x30 -> x29, local copies, waits for them, and re-layouts: 11 us -> 9.54 us
  transfers between devices with their start and end apart: 16 -> 16, of which waited for: 13 -> 11; matrix products, arithmetic and copies ran while one was open for 10% -> 13% of each run, Pallas kernels for 0% -> 0%
where the time goes in v1:
time: 245 us; the launch traced here: 244 us
  waiting for transfers between devices  168 us (69%)
  other arithmetic  24.3 us (10%)
  starting transfers between devices  15.1 us (6%)
  between operations  14.3 us (6%)
  local copies, waits for them, and re-layouts  13.7 us (6%)
  matrix products  8.93 us (4%)
    ppermute x12, waiting for transfers between devices, swapped(): return lax.ppermute(block, axis, route)  121 us
    reduce_scatter x1, waiting for transfers between devices, on_device(): lax.psum_scatter(weight_term, 'seq', scatter_dimension=0, tiled=True)  46.1 us
    ppermute x12, starting transfers between devices, swapped(): return lax.ppermute(block, axis, route)  12.7 us
    unnamed x29, local copies, waits for them, and re-layouts  9.54 us
    convert_element_type x4, other arithmetic, mix_adjoint(): state = jnp.where(upper_side, as_upper, as_lower).astype(jnp.bfloat16)  8.65 us
    convert_element_type x5, other arithmetic, mix_forward(): state = jnp.where(upper_side, as_upper, as_lower).astype(jnp.bfloat16)  7.59 us
    convert_element_type x2, other arithmetic, layer_forward(): (rows.astype(jnp.float32) + state.astype(jnp.float32)).astype(jnp.bfloat16)  5.91 us
  transfers between devices with their start and end apart: 16, of which 11 were waited for; matrix products, arithmetic and copies ran while one was open for 13% of the time, Pallas kernels for 0%

profile of v1, /device:TPU:0, one launch (start us, length us, event | category | flops | bytes accessed | tf_op | source)
XLA Modules:
  0.0 243.9 jit_solution(2915484954091573407)
XLA Ops:
  7.2 0.7 copy-done
  7.9 1.3 fusion.1
  9.3 0.5 collective-permute-start.6
  9.8 1.4 slice_reduce_fusion.15
  11.2 1.4 fusion.20
  12.6 2.9 %collective-permute-start.7 = (bf16[128,1792]{0,1:T(8,128)(2,1)S(1)}, bf16[128,1792]{0,1:T(8,128)(2,1)S(1)}, u32[]{:S(2)}, u32[]{:S(2)}) collective-permute-start(bf16[128,1792]{0,1:T(8,128)(2,1)S(1)} %fusion.20), channel_id=1, source_target_pairs={{0,2},{2,0},{1,3},{3,1},{4,6},{6,4},{5,7},{7,5},{8,10},{10,8},{9,1... | collective-permute-start | bytes 1376264 | tf_op jit(solution)/shard_map/ppermute | solution.py:19
  15.5 10.9 %collective-permute-done.7 = bf16[128,1792]{0,1:T(8,128)(2,1)S(1)} collective-permute-done((bf16[128,1792]{0,1:T(8,128)(2,1)S(1)}, bf16[128,1792]{0,1:T(8,128)(2,1)S(1)}, u32[]{:S(2)}, u32[]{:S(2)}) %collective-permute-start.7) | collective-permute-done | bytes 458784 | tf_op jit(solution)/shard_map/ppermute | solution.py:19
  26.4 1.3 fusion.24
  27.7 1.9 collective-permute-start.8
  29.6 10.3 %collective-permute-done.8 = bf16[128,1792]{0,1:T(8,128)(2,1)S(1)} collective-permute-done((bf16[128,1792]{0,1:T(8,128)(2,1)S(1)}, bf16[128,1792]{0,1:T(8,128)(2,1)S(1)}, u32[]{:S(2)}, u32[]{:S(2)}) %collective-permute-start.8) | collective-permute-done | bytes 458784 | tf_op jit(solution)/shard_map/ppermute | solution.py:19
  39.9 1.3 fusion.28
  41.3 2.6 %collective-permute-start.9 = (bf16[128,1792]{0,1:T(8,128)(2,1)S(1)}, bf16[128,1792]{0,1:T(8,128)(2,1)}, u32[]{:S(2)}, u32[]{:S(2)}) collective-permute-start(bf16[128,1792]{0,1:T(8,128)(2,1)S(1)} %fusion.28), channel_id=1, source_target_pairs={{0,8},{8,0},{1,9},{9,1},{2,10},{10,2},{3,11},{11,3},{4,12},{12,4},... | collective-permute-start | bytes 1376264 | tf_op jit(solution)/shard_map/ppermute | solution.py:19
  43.8 1.0 copy.12
  44.8 1.5 collective-permute-start.5
  46.3 1.0 copy.13
  47.3 2.8 %copy.18 = bf16[1,1792,448]{2,1,0:T(8,128)(2,1)S(1)} copy(bf16[1,1792,448]{1,2,0:T(8,128)(2,1)} %param.11) | data formatting | bytes 3211264 | tf_op jit(solution)/shard_map/reshape;squeeze | solution.py:71
  50.0 13.3 %collective-permute-done.9 = bf16[128,1792]{0,1:T(8,128)(2,1)} collective-permute-done((bf16[128,1792]{0,1:T(8,128)(2,1)S(1)}, bf16[128,1792]{0,1:T(8,128)(2,1)}, u32[]{:S(2)}, u32[]{:S(2)}) %collective-permute-start.9) | collective-permute-done | bytes 458784 | tf_op jit(solution)/shard_map/ppermute | solution.py:19
  63.4 3.0 %add_convert_fusion.1 = bf16[128,1792]{0,1:T(8,128)(2,1)S(1)} fusion(bf16[128,1792]{0,1:T(8,128)(2,1)} %copy-done.10, bf16[128,1792]{0,1:T(8,128)(2,1)} %collective-permute-done.9, bf16[1,128,1792]{1,2,0:T(8,128)(2,1)} %copy.13, f32[1792]{0:T(1024)S(1)} %get-tuple-element.9, f32[1792]{0:T(1024)S(1)} %get-tuple-element.10, f32[1792]{0:T(1024)S(1)} %get-tuple-element.11, ...), kind=kLoop, calls=%fused_computation.109 | loop fusion | flops 3211264 | bytes 1863681 | tf_op jit(solution)/shard_map/convert_element_type | solution.py:69
  66.4 0.8 convolution_bitcast_fusion.1
  67.2 0.7 fusion.60
  68.1 0.9 copy-done.4
  69.3 22.5 %collective-permute-done.10 = bf16[128,1792]{0,1:T(8,128)(2,1)S(1)} collective-permute-done((bf16[128,1792]{0,1:T(8,128)(2,1)S(1)}, bf16[128,1792]{0,1:T(8,128)(2,1)S(1)}, u32[]{:S(2)}, u32[]{:S(2)}) %collective-permute-start.10) | collective-permute-done | bytes 458784 | tf_op jit(solution)/shard_map/ppermute | solution.py:19
  91.8 2.2 fusion.36
  94.0 2.0 copy.10
  96.0 0.6 collective-permute-start
  96.6 9.1 %collective-permute-done.11 = bf16[128,1792]{0,1:T(8,128)(2,1)} collective-permute-done((bf16[128,1792]{0,1:T(8,128)(2,1)}, bf16[128,1792]{0,1:T(8,128)(2,1)}, u32[]{:S(2)}, u32[]{:S(2)}) %collective-permute-start.11) | collective-permute-done | bytes 458784 | tf_op jit(solution)/shard_map/ppermute | solution.py:19
  105.7 2.9 %fusion.40 = bf16[128,1792]{0,1:T(8,128)(2,1)S(1)} fusion(bf16[128,1792]{0,1:T(8,128)(2,1)} %collective-permute-done.11, bf16[128,1792]{0,1:T(8,128)(2,1)} %fusion.36, f32[1792]{0:T(1024)S(1)} %get-tuple-element.12, f32[1792]{0:T(1024)S(1)} %get-tuple-element.13, f32[1792]{0:T(1024)S(1)} %get-tuple-element.14, f32[1792]{0:T(1024)S(1)} %get-tuple-element.23, ...), kind=kLoop, calls=%fused_computation.93 | loop fusion | flops 2293760 | bytes 1404929 | tf_op jit(solution)/shard_map/convert_element_type | solution.py:52
  109.0 10.0 %collective-permute-done.12 = bf16[128,1792]{0,1:T(8,128)(2,1)S(1)} collective-permute-done((bf16[128,1792]{0,1:T(8,128)(2,1)S(1)}, bf16[128,1792]{0,1:T(8,128)(2,1)S(1)}, u32[]{:S(2)}, u32[]{:S(2)}) %collective-permute-start.12) | collective-permute-done | bytes 458784 | tf_op jit(solution)/shard_map/ppermute | solution.py:19
  119.0 1.3 fusion.44
  120.5 1.8 collective-permute-done.13
  122.2 2.2 fusion.48
  124.5 0.8 copy-done.2
  125.2 1.0 fusion.52
  126.5 3.7 %fusion.59 = f32[4,448,448]{2,1,0:T(8,128)} fusion(bf16[128,4,448]{0,2,1:T(8,128)(2,1)S(1)} %bitcast.83, f32[128,4,448]{0,2,1:T(8,128)} %copy-done.6, bf16[128,4,448]{0,2,1:T(8,128)(2,1)S(1)} %bitcast.81), kind=kOutput, calls=%fused_computation.135 | convolution fusion | flops 207814656 | bytes 5046272 | tf_op jit(solution)/shard_map/tbi,tbo->bio/dot_general | solution.py:100
  130.2 1.0 copy-done.9
  131.4 13.0 %collective-permute-done.2 = bf16[128,1792]{0,1:T(8,128)(2,1)S(1)} collective-permute-done((bf16[128,1792]{0,1:T(8,128)(2,1)S(1)}, bf16[128,1792]{0,1:T(8,128)(2,1)S(1)}, u32[]{:S(2)}, u32[]{:S(2)}) %collective-permute-start.2) | collective-permute-done | bytes 458784 | tf_op jit(solution)/shard_map/ppermute | solution.py:19
  144.4 1.3 fusion.8
  145.8 0.6 collective-permute-start.3
  146.7 13.9 %collective-permute-done.3 = bf16[128,1792]{0,1:T(8,128)(2,1)S(1)} collective-permute-done((bf16[128,1792]{0,1:T(8,128)(2,1)S(1)}, bf16[128,1792]{0,1:T(8,128)(2,1)S(1)}, u32[]{:S(2)}, u32[]{:S(2)}) %collective-permute-start.3) | collective-permute-done | bytes 458784 | tf_op jit(solution)/shard_map/ppermute | solution.py:19
  160.6 2.2 fusion.12
  162.8 3.7 %collective-permute-start.4 = (bf16[128,1792]{0,1:T(8,128)(2,1)}, bf16[128,1792]{0,1:T(8,128)(2,1)}, u32[]{:S(2)}, u32[]{:S(2)}) collective-permute-start(bf16[128,1792]{0,1:T(8,128)(2,1)} %fusion.12), channel_id=1, source_target_pairs={{0,8},{8,0},{1,9},{9,1},{2,10},{10,2},{3,11},{11,3},{4,12},{12,4},... | collective-permute-start | bytes 1376264 | tf_op jit(solution)/shard_map/ppermute | solution.py:19
  166.6 1.0 copy.17
  167.6 16.7 %collective-permute-done.4 = bf16[128,1792]{0,1:T(8,128)(2,1)} collective-permute-done((bf16[128,1792]{0,1:T(8,128)(2,1)}, bf16[128,1792]{0,1:T(8,128)(2,1)}, u32[]{:S(2)}, u32[]{:S(2)}) %collective-permute-start.4) | collective-permute-done | bytes 458784 | tf_op jit(solution)/shard_map/ppermute | solution.py:19
  184.3 2.9 %add_convert_fusion.3 = bf16[128,1792]{0,1:T(8,128)(2,1)S(1)} fusion(bf16[128,1792]{0,1:T(8,128)(2,1)} %fusion.12, bf16[128,1792]{0,1:T(8,128)(2,1)} %collective-permute-done.4, bf16[1,128,1792]{1,2,0:T(8,128)(2,1)S(1)} %copy-done.8, f32[1792]{0:T(1024)S(1)} %get-tuple-element.9, f32[1792]{0:T(1024)S(1)} %get-tuple-element.10, ...), kind=kLoop, calls=%fused_computation.111 | loop fusion | flops 3211264 | bytes 1863681 | tf_op jit(solution)/shard_map/convert_element_type | solution.py:69
  187.3 0.9 add_convert_fusion.2
  188.1 1.0 copy.16
  189.1 1.9 reduce_sum.9
  191.0 46.1 %reduce-scatter.2.cloned.1.call-done = f32[112,448]{1,0:T(8,128)} async-done(((f32[1792,448]{1,0:T(8,128)}), f32[112,448]{1,0:T(8,128)}) %reduce-scatter.2.cloned.1.call-update) | async-done | bytes 200720 | tf_op jit(solution)/shard_map/reduce_scatter | solution.py:103
  (39 shorter events, 1.9 us)
Async XLA Ops:
  7.2 0.8 copy-start
  7.2 181.9 %all-gather.3.cloned.1.call-start = ((), (), s32[]{:S(2)}) async-start(), calls=%async_computation.2 | async-start | bytes 1114112 | tf_op jit(solution)/shard_map/all_gather | solution.py:8
  9.3 2.0 collective-permute-start.6
  11.2 32.6 %copy-start.11 = (bf16[1,128,1792]{2,1,0:T(8,128)(2,1)S(1)}, bf16[1,128,1792]{2,1,0:T(8,128)(2,1)}, u32[]{:S(2)}) copy-start(bf16[1,128,1792]{2,1,0:T(8,128)(2,1)} %param.7) | copy-start | bytes 1376260
  12.6 13.8 %collective-permute-start.7 = (bf16[128,1792]{0,1:T(8,128)(2,1)S(1)}, bf16[128,1792]{0,1:T(8,128)(2,1)S(1)}, u32[]{:S(2)}, u32[]{:S(2)}) collective-permute-start(bf16[128,1792]{0,1:T(8,128)(2,1)S(1)} %fusion.20), channel_id=1, source_target_pairs={{0,2},{2,0},{1,3},{3,1},{4,6},{6,4},{5,7},{7,5},{8,10},{10,8},{9,1... | collective-permute-start | bytes 1376264 | tf_op jit(solution)/shard_map/ppermute | solution.py:19
  26.4 19.9 %copy-start.1 = (bf16[1,128,1792]{2,1,0:T(8,128)(2,1)S(1)}, bf16[1,128,1792]{2,1,0:T(8,128)(2,1)}, u32[]{:S(2)}) copy-start(bf16[1,128,1792]{2,1,0:T(8,128)(2,1)} %param.8) | copy-start | bytes 1376260
  27.7 12.2 %collective-permute-start.8 = (bf16[128,1792]{0,1:T(8,128)(2,1)S(1)}, bf16[128,1792]{0,1:T(8,128)(2,1)S(1)}, u32[]{:S(2)}, u32[]{:S(2)}) collective-permute-start(bf16[128,1792]{0,1:T(8,128)(2,1)S(1)} %fusion.24), channel_id=1, source_target_pairs={{0,4},{4,0},{1,5},{5,1},{2,6},{6,2},{3,7},{7,3},{8,12},{12,8},{9,1... | collective-permute-start | bytes 1376264 | tf_op jit(solution)/shard_map/ppermute | solution.py:19
  41.2 8.8 %copy-start.10 = (bf16[128,1792]{0,1:T(8,128)(2,1)}, bf16[128,1792]{0,1:T(8,128)(2,1)S(1)}, u32[]{:S(2)}) copy-start(bf16[128,1792]{0,1:T(8,128)(2,1)S(1)} %fusion.28) | copy-start | bytes 1376260
  41.3 22.1 %collective-permute-start.9 = (bf16[128,1792]{0,1:T(8,128)(2,1)S(1)}, bf16[128,1792]{0,1:T(8,128)(2,1)}, u32[]{:S(2)}, u32[]{:S(2)}) collective-permute-start(bf16[128,1792]{0,1:T(8,128)(2,1)S(1)} %fusion.28), channel_id=1, source_target_pairs={{0,8},{8,0},{1,9},{9,1},{2,10},{10,2},{3,11},{11,3},{4,12},{12,4},... | collective-permute-start | bytes 1376264 | tf_op jit(solution)/shard_map/ppermute | solution.py:19
  44.8 22.4 %collective-permute-start.5 = (bf16[1,128,1792]{1,2,0:T(8,128)(2,1)}, bf16[1,128,1792]{1,2,0:T(8,128)(2,1)S(1)}, u32[]{:S(2)}, u32[]{:S(2)}) collective-permute-start(bf16[1,128,1792]{1,2,0:T(8,128)(2,1)} %copy.12), channel_id=1, source_target_pairs={{16,0},{0,16},{17,1},{1,17},{18,2},{2,18},{19,3},{3,19},{20,4},{4,... | collective-permute-start | bytes 1376264 | tf_op jit(solution)/shard_map/ppermute | solution.py:25
  67.2 0.9 copy-start.6
  68.1 0.9 copy-start.4
  69.2 22.6 %collective-permute-start.10 = (bf16[128,1792]{0,1:T(8,128)(2,1)S(1)}, bf16[128,1792]{0,1:T(8,128)(2,1)S(1)}, u32[]{:S(2)}, u32[]{:S(2)}) collective-permute-start(bf16[128,1792]{0,1:T(8,128)(2,1)S(1)} %fusion.50), channel_id=1, source_target_pairs={{0,8},{8,0},{1,9},{9,1},{2,10},{10,2},{3,11},{11,3},{4,12},{12,4},... | collective-permute-start | bytes 1376264 | tf_op jit(solution)/shard_map/ppermute | solution.py:19
  94.0 11.6 %collective-permute-start.11 = (bf16[128,1792]{0,1:T(8,128)(2,1)}, bf16[128,1792]{0,1:T(8,128)(2,1)}, u32[]{:S(2)}, u32[]{:S(2)}) collective-permute-start(bf16[128,1792]{0,1:T(8,128)(2,1)} %fusion.36), channel_id=1, source_target_pairs={{0,4},{4,0},{1,5},{5,1},{2,6},{6,2},{3,7},{7,3},{8,12},{12,8},{9,1... | collective-permute-start | bytes 1376264 | tf_op jit(solution)/shard_map/ppermute | solution.py:19
  96.0 12.6 %collective-permute-start = (bf16[1,128,1792]{1,2,0:T(8,128)(2,1)}, bf16[1,128,1792]{1,2,0:T(8,128)(2,1)S(1)}, u32[]{:S(2)}, u32[]{:S(2)}) collective-permute-start(bf16[1,128,1792]{1,2,0:T(8,128)(2,1)} %copy.10), channel_id=1, source_target_pairs={{16,0},{0,16},{17,1},{1,17},{18,2},{2,18},{19,3},{3,19},{20,4},{4,... | collective-permute-start | bytes 1376264 | tf_op jit(solution)/shard_map/ppermute | solution.py:25
  108.5 10.5 %collective-permute-start.12 = (bf16[128,1792]{0,1:T(8,128)(2,1)S(1)}, bf16[128,1792]{0,1:T(8,128)(2,1)S(1)}, u32[]{:S(2)}, u32[]{:S(2)}) collective-permute-start(bf16[128,1792]{0,1:T(8,128)(2,1)S(1)} %fusion.40), channel_id=1, source_target_pairs={{0,2},{2,0},{1,3},{3,1},{4,6},{6,4},{5,7},{7,5},{8,10},{10,8},{9,1... | collective-permute-start | bytes 1376264 | tf_op jit(solution)/shard_map/ppermute | solution.py:19
  108.6 11.8 %copy-start.7 = (bf16[1,128,1792]{1,2,0:T(8,128)(2,1)}, bf16[1,128,1792]{1,2,0:T(8,128)(2,1)S(1)}, u32[]{:S(2)}) copy-start(bf16[1,128,1792]{1,2,0:T(8,128)(2,1)S(1)} %collective-permute-done) | copy-start | bytes 1376260
  108.9 11.5 %collective-permute-start.1 = (bf16[128,1792]{0,1:T(8,128)(2,1)S(1)}, bf16[128,1792]{0,1:T(8,128)(2,1)S(1)}, u32[]{:S(2)}, u32[]{:S(2)}) collective-permute-start(bf16[128,1792]{0,1:T(8,128)(2,1)S(1)} %fusion), channel_id=1, source_target_pairs={{0,1},{1,0},{2,3},{3,2},{4,5},{5,4},{6,7},{7,6},{8,9},{9,8},{10,11... | collective-permute-start | bytes 1376264 | tf_op jit(solution)/shard_map/ppermute | solution.py:19
  120.4 1.9 collective-permute-start.13
  124.5 0.8 copy-start.2
  126.2 110.9 %reduce-scatter.2.cloned.1.call-start = ((), (), s32[]{:S(2)}) async-start(), calls=%async_computation.1 | async-start | bytes 3899392 | tf_op jit(solution)/shard_map/reduce_scatter | solution.py:103
  130.1 1.0 copy-start.9
  130.1 16.3 %copy-start.3 = (bf16[128,1792]{0,1:T(8,128)(2,1)S(1)}, bf16[128,1792]{0,1:T(8,128)(2,1)}, u32[]{:S(2)}) copy-start(bf16[128,1792]{0,1:T(8,128)(2,1)} %copy-done.2) | copy-start | bytes 1376260
  131.2 35.3 %copy-start.5 = (f32[4,128,448]{1,2,0:T(8,128)S(1)}, f32[4,128,448]{1,2,0:T(8,128)}, u32[]{:S(2)}) copy-start(f32[4,128,448]{1,2,0:T(8,128)} %copy-done.4) | copy-start | bytes 2752516
  131.2 13.3 %collective-permute-start.2 = (bf16[128,1792]{0,1:T(8,128)(2,1)S(1)}, bf16[128,1792]{0,1:T(8,128)(2,1)S(1)}, u32[]{:S(2)}, u32[]{:S(2)}) collective-permute-start(bf16[128,1792]{0,1:T(8,128)(2,1)S(1)} %copy-done.9), channel_id=1, source_target_pairs={{0,2},{2,0},{1,3},{3,1},{4,6},{6,4},{5,7},{7,5},{8,10},{10,8},{9,1... | collective-permute-start | bytes 1376264 | tf_op jit(solution)/shard_map/ppermute | solution.py:19
  145.8 14.8 %collective-permute-start.3 = (bf16[128,1792]{0,1:T(8,128)(2,1)S(1)}, bf16[128,1792]{0,1:T(8,128)(2,1)S(1)}, u32[]{:S(2)}, u32[]{:S(2)}) collective-permute-start(bf16[128,1792]{0,1:T(8,128)(2,1)S(1)} %fusion.8), channel_id=1, source_target_pairs={{0,4},{4,0},{1,5},{5,1},{2,6},{6,2},{3,7},{7,3},{8,12},{12,8},{9,1... | collective-permute-start | bytes 1376264 | tf_op jit(solution)/shard_map/ppermute | solution.py:19
  162.8 21.6 %collective-permute-start.4 = (bf16[128,1792]{0,1:T(8,128)(2,1)}, bf16[128,1792]{0,1:T(8,128)(2,1)}, u32[]{:S(2)}, u32[]{:S(2)}) collective-permute-start(bf16[128,1792]{0,1:T(8,128)(2,1)} %fusion.12), channel_id=1, source_target_pairs={{0,8},{8,0},{1,9},{9,1},{2,10},{10,2},{3,11},{11,3},{4,12},{12,4},... | collective-permute-start | bytes 1376264 | tf_op jit(solution)/shard_map/ppermute | solution.py:19
  166.5 17.9 %copy-start.8 = (bf16[1,128,1792]{1,2,0:T(8,128)(2,1)S(1)}, bf16[1,128,1792]{1,2,0:T(8,128)(2,1)}, u32[]{:S(2)}) copy-start(bf16[1,128,1792]{1,2,0:T(8,128)(2,1)} %copy-done.7) | copy-start | bytes 1376260
Sparse Core Ops, SparseCore 0:
  126.3 38.7 all-gather.2
  169.5 67.5 reduce-scatter.1
